TPU v7x, 32 devices: a whole 2x2x4 slice. The times are simulated.
32 devices in a mesh: seq: 8 (over y, x, core), head: 4 (over z).
Axes of the slice: x: 2, y: 2, z: 4, core: 2. Of those that a mesh axis runs over, the one named last changes fastest.
Arguments:
- queries: bfloat16 [1280, 64, 128], P(('seq', 'head')), may hold values from -8 to 8
- key_one: bfloat16 [1280, 128], P(('seq', 'head')), may hold values from -6 to 6
- value_one: bfloat16 [1280, 128], P(('seq', 'head')), may hold values from -6 to 6
- key_two: bfloat16 [1280, 128], P(('seq', 'head')), may hold values from -6 to 6
- value_two: bfloat16 [1280, 128], P(('seq', 'head')), may hold values from -6 to 6
Outputs:
- attended: bfloat16 [1280, 64, 128], P(('seq', 'head'))
All inputs are finite; a program needn't handle non-finite values.
Results may differ from a plain program's by a relative error of at most 0.0058.
Values may be sent and summed in bfloat16 or wider, within the bound.
A program may use at most 64 MiB of HBM per device.

v0:
```python
import math

import jax
import jax.numpy as jnp
from jax import lax
from jax.sharding import PartitionSpec as P

WIN_ONE = 512
WIN_TWO = 32


def from_behind(shard, axis, by):
    count = lax.axis_size(axis)
    pairs = [(i, i + by) for i in range(count) if 0 <= i + by < count]
    return lax.ppermute(shard, axis, pairs)


def window_attend(query_rows, keys_one, values_one, keys_two, values_two, first_pos):
    block_rows, group_size, head_depth = query_rows.shape
    width_two = keys_two.shape[0] - block_rows + 1
    width_one = keys_one.shape[0] - block_rows + 1
    key_span = keys_one.shape[0]
    near_keys = jnp.stack(
        [
            keys_two[width_two - 1 - offset : width_two - 1 - offset + block_rows]
            for offset in range(width_two)
        ],
        axis=1,
    )
    near_values = jnp.stack(
        [
            values_two[width_two - 1 - offset : width_two - 1 - offset + block_rows]
            for offset in range(width_two)
        ],
        axis=1,
    )
    score_scale = 1.0 / math.sqrt(head_depth)
    product = (
        query_rows.astype(jnp.float32)[:, :, None, :]
        * near_keys.astype(jnp.float32)[:, None, :, :]
        * score_scale
    ).astype(jnp.bfloat16)
    logits = lax.dot_general(
        product.reshape(-1, head_depth),
        keys_one,
        (((1,), (1,)), ((), ())),
        preferred_element_type=jnp.float32,
    )
    logits = logits.reshape(block_rows, group_size, width_two, key_span)
    row_pos = lax.broadcasted_iota(jnp.int32, (block_rows, 1, 1, 1), 0)
    lag_pos = lax.broadcasted_iota(jnp.int32, (1, 1, width_two, 1), 2)
    col_pos = lax.broadcasted_iota(jnp.int32, (1, 1, 1, key_span), 3)
    inside = (col_pos >= row_pos) & (col_pos <= row_pos + width_one - 1)
    inside = (
        inside & (first_pos - width_one + 1 + col_pos >= 0) & (first_pos + row_pos - lag_pos >= 0)
    )
    logits = jnp.where(inside, logits, -1e30)
    peak_value = jnp.max(logits, axis=(2, 3), keepdims=True)
    raised = jnp.exp(logits - peak_value)
    weights = (raised / jnp.sum(raised, axis=(2, 3), keepdims=True)).astype(jnp.bfloat16)
    blended = jnp.dot(weights.reshape(-1, key_span), values_one, preferred_element_type=jnp.float32)
    blended = blended.reshape(block_rows, group_size, width_two, head_depth)
    return jnp.sum(blended * near_values.astype(jnp.float32)[:, None, :, :], axis=2)


def preceding(arrays, reach_count):
    earlier = []
    current = arrays
    for distance in range(reach_count):
        current = from_behind((current[0], current[1]), "seq", 1)
        earlier.append(current)
    return earlier[::-1]


def second_rim(arrays):
    return from_behind((arrays[0], arrays[1]), "seq", 1)


def body(queries, key_one, value_one, key_two, value_two):
    group_count = lax.axis_size("head")
    piece_rows = key_one.shape[0]
    head_depth = key_one.shape[1]
    shard_rows = piece_rows * group_count
    reach_count = (WIN_ONE - 1) // shard_rows + 1
    earlier = preceding((key_one, value_one), reach_count)
    rim_keys, rim_values = second_rim((key_two, value_two))
    stack_keys_one = jnp.stack([pair[0] for pair in earlier] + [key_one], axis=0)
    stack_values_one = jnp.stack([pair[1] for pair in earlier] + [value_one], axis=0)
    stack_keys_two = jnp.stack([rim_keys, key_two], axis=0)
    stack_values_two = jnp.stack([rim_values, value_two], axis=0)
    whole_k1, whole_v1, whole_k2, whole_v2 = (
        lax.all_gather(stack_keys_one, "head", axis=1, tiled=True),
        lax.all_gather(stack_values_one, "head", axis=1, tiled=True),
        lax.all_gather(stack_keys_two, "head", axis=1, tiled=True),
        lax.all_gather(stack_values_two, "head", axis=1, tiled=True),
    )
    first_keys = whole_k1.reshape(-1, head_depth)
    first_values = whole_v1.reshape(-1, head_depth)
    second_keys = whole_k2.reshape(-1, head_depth)
    second_values = whole_v2.reshape(-1, head_depth)
    shard_first = lax.axis_index("seq") * shard_rows
    query_split = queries.reshape(piece_rows, group_count, -1, head_depth)
    grouped = lax.all_to_all(query_split, "head", split_axis=1, concat_axis=0, tiled=True)[:, 0]
    row_count = grouped.shape[0]
    block_rows = math.gcd(row_count, 16)

    def attend(index):
        local_start = index * block_rows
        query_rows = lax.dynamic_slice_in_dim(grouped, local_start, block_rows, 0)
        begin_one = reach_count * shard_rows + local_start - WIN_ONE + 1
        begin_two = shard_rows + local_start - WIN_TWO + 1
        keys_one = lax.dynamic_slice_in_dim(first_keys, begin_one, block_rows + WIN_ONE - 1, 0)
        values_one = lax.dynamic_slice_in_dim(first_values, begin_one, block_rows + WIN_ONE - 1, 0)
        keys_two = lax.dynamic_slice_in_dim(second_keys, begin_two, block_rows + WIN_TWO - 1, 0)
        values_two = lax.dynamic_slice_in_dim(second_values, begin_two, block_rows + WIN_TWO - 1, 0)
        return window_attend(
            query_rows, keys_one, values_one, keys_two, values_two, shard_first + local_start
        ).astype(jnp.bfloat16)

    blocks = lax.map(attend, jnp.arange(row_count // block_rows, dtype=jnp.int32))
    result = blocks.reshape(row_count, grouped.shape[1], head_depth).reshape(
        shard_rows, 1, grouped.shape[1], head_depth
    )
    outputs = lax.all_to_all(result, "head", split_axis=0, concat_axis=1, tiled=True)
    return outputs.reshape(piece_rows, -1, head_depth)


def solution(mesh):
    placed = (
        P(("seq", "head"), None, None),
        P(("seq", "head"), None),
        P(("seq", "head"), None),
        P(("seq", "head"), None),
        P(("seq", "head"), None),
    )
    return jax.shard_map(
        body, mesh=mesh, in_specs=placed, out_specs=P(("seq", "head"), None, None), check_vma=False
    )
```

profile of v0, /device:TPU:4, one launch (start us, length us, event | category | flops | bytes accessed | tf_op | source)
XLA Modules:
  0.0 311.3 jit_solution(15725463585320559232)
XLA Ops:
  0.0 1.9 collective-permute-start
  1.9 3.5 %collective-permute-start.1 = (bf16[40,128]{1,0:T(8,128)(2,1)}, bf16[40,128]{1,0:T(8,128)(2,1)S(1)}, u32[]{:S(2)}, u32[]{:S(2)}) collective-permute-start(bf16[40,128]{1,0:T(8,128)(2,1)} %param.8), channel_id=1, source_target_pairs={{0,4},{4,8},{8,12},{12,16},{16,20},{20,24},{24,28},{1,5},{5,9},{9,... | collective-permute-start | bytes 30728 | tf_op jit(solution)/shard_map/ppermute | solution.py:15
  5.4 1.9 collective-permute-start.5
  7.4 2.0 copy.18
  9.4 4.9 %all-to-all-start = ((bf16[40,4,16,128]{3,2,0,1:T(8,128)(2,1)}), bf16[40,4,16,128]{3,2,0,1:T(8,128)(2,1)S(1)}, u32[]{:S(2)}, u32[]{:S(2)}) async-start(bf16[40,4,16,128]{3,2,0,1:T(8,128)(2,1)} %copy.18), calls=%async_computation | async-start | bytes 1310720 | tf_op jit(solution)/shard_map/all_to_all | solution.py:103
  14.3 1.9 collective-permute-start.9
  16.2 0.7 pad_maximum_fusion
  16.9 1.9 collective-permute-start.2
  18.8 1.5 collective-permute-done.9
  20.4 0.7 pad_maximum_fusion.1
  21.1 1.9 collective-permute-start.6
  23.0 1.9 collective-permute-start.3
  24.9 13.9 %all_gather.12 = bf16[2,160,128]{2,1,0:T(8,128)(2,1)S(1)} all-gather(bf16[2,40,128]{2,1,0:T(8,128)(2,1)S(1)} %pad_maximum_fusion), channel_id=1, replica_groups=mesh['seq'=8,'head'=4] {'head'}, dimensions={1}, use_global_device_ids=true | all-gather | bytes 102400 | tf_op jit(solution)/shard_map/all_gather | solution.py:94
  38.8 1.9 collective-permute-start.7
  40.7 1.9 collective-permute-start.4
  42.7 13.2 %all_gather.15 = bf16[2,160,128]{2,1,0:T(8,128)(2,1)S(1)} all-gather(bf16[2,40,128]{2,1,0:T(8,128)(2,1)S(1)} %pad_maximum_fusion.1), channel_id=1, replica_groups=mesh['seq'=8,'head'=4] {'head'}, dimensions={1}, use_global_device_ids=true | all-gather | bytes 102400 | tf_op jit(solution)/shard_map/all_gather | solution.py:95
  55.9 1.9 collective-permute-start.8
  57.8 0.7 constant_dynamic-update-slice_fusion.64
  58.6 3.2 %collective-permute-done.8 = bf16[40,128]{1,0:T(8,128)(2,1)S(1)} collective-permute-done((bf16[40,128]{1,0:T(8,128)(2,1)S(1)}, bf16[40,128]{1,0:T(8,128)(2,1)S(1)}, u32[]{:S(2)}, u32[]{:S(2)}) %collective-permute-start.8) | collective-permute-done | bytes 10272 | tf_op jit(solution)/shard_map/ppermute | solution.py:15
  61.8 14.1 %all_gather.13 = bf16[5,160,128]{2,1,0:T(8,128)(2,1)S(1)} all-gather(bf16[5,40,128]{2,1,0:T(8,128)(2,1)S(1)} %constant_dynamic-update-slice_fusion.64), channel_id=1, replica_groups=mesh['seq'=8,'head'=4] {'head'}, dimensions={1}, use_global_device_ids=true | all-gather | bytes 256000 | tf_op jit(solution)/shard_map/all_gather | solution.py:92
  75.8 0.7 constant_dynamic-update-slice_fusion.69
  76.6 13.6 %all_gather.14 = bf16[5,160,128]{2,1,0:T(8,128)(2,1)S(1)} all-gather(bf16[5,40,128]{2,1,0:T(8,128)(2,1)S(1)} %constant_dynamic-update-slice_fusion.69), channel_id=1, replica_groups=mesh['seq'=8,'head'=4] {'head'}, dimensions={1}, use_global_device_ids=true | all-gather | bytes 256000 | tf_op jit(solution)/shard_map/all_gather | solution.py:93
  90.2 204.2 %while.15 = (s32[]{:T(128)}, bf16[10,16,16,128]{3,2,1,0:T(8,128)(2,1)S(1)}, s32[10]{0:T(128)S(1)}, s32[]{:T(128)}, bf16[160,16,128]{2,1,0:T(8,128)(2,1)S(1)}, /*...) while((s32[]{:T(128)}, ...), condition=%wide.region_4.5_spmd, body=%wide.region_0.4_spmd.sunk | while | flops 2254800896 | bytes 59373492 | solution.py:120
  90.2 0.6 dynamic_slice.79
  93.6 3.3 %select_reduce_fusion.2 = (f32[16,16]{1,0:T(8,128)S(1)}, f32[16,16,32,527]{3,2,1,0:T(8,128)S(1)}) fusion(pred[16,32,527]{2,1,0:T(8,128)(4,1)S(1)} %broadcast_and_fusion.2, bf16[800,128]{1,0:T(8,128)(2,1)S(1)} %get-tuple-element.416, s32[]{:T(128)S(6)} %select_n.62, f32[16,32,128]{2,1,0:T(8,128)S(1)} %copy.25, ...), kind=kOutput, calls=%fused_computation.2.clone.1 | convolution fusion | flops 1116978944 | bytes 18125828 | tf_op jit(solution)/shard_map/while/body/eval_jaxpr/dot_general | solution.py:43
  96.8 8.4 %fusion.85 = f32[16,16]{1,0:T(8,128)S(1)} fusion(f32[16,16,32,527]{3,2,1,0:T(8,128)S(1)} %get-tuple-element.312, f32[16,16]{1,0:T(8,128)S(1)} %get-tuple-element.313, pred[16,32,527]{2,1,0:T(8,128)(4,1)S(1)} %broadcast_and_fusion.2), kind=kLoop, calls=%fused_computation.3.clone.1 | loop fusion | flops 12951296 | bytes 17540608 | tf_op jit(solution)/shard_map/while/body/eval_jaxpr/reduce_sum | solution.py:60
  105.3 5.3 %multiply_reduce_fusion.2 = bf16[16,16,128]{2,1,0:T(8,128)(2,1)S(1)} fusion(f32[16,32,128]{2,1,0:T(8,128)S(1)} %copy.24, f32[16,16,32,527]{3,2,1,0:T(8,128)S(1)} %get-tuple-element.312, f32[16,16]{1,0:T(8,128)S(1)} %fusion.85, f32[16,16]{1,0:T(8,128)S(1)} %get-tuple-element.313, pred[16,32,527]{2,1,0:T(8,128)(4,1)S(1)} %broadcast_and_fusion.2, ...), kind=kOutput, calls=%fused_computation.5.clone.1 | convolution fusion | flops 1124532224 | bytes 21778436 | tf_op jit(solution)/shard_map/while/body/eval_jaxpr/dot_general | solution.py:61
  110.6 0.6 dynamic_slice.79
  114.0 3.3 %select_reduce_fusion.2 = (f32[16,16]{1,0:T(8,128)S(1)}, f32[16,16,32,527]{3,2,1,0:T(8,128)S(1)}) fusion(pred[16,32,527]{2,1,0:T(8,128)(4,1)S(1)} %broadcast_and_fusion.2, bf16[800,128]{1,0:T(8,128)(2,1)S(1)} %get-tuple-element.416, s32[]{:T(128)S(6)} %select_n.62, f32[16,32,128]{2,1,0:T(8,128)S(1)} %copy.25, ...), kind=kOutput, calls=%fused_computation.2.clone.1 | convolution fusion | flops 1116978944 | bytes 18125828 | tf_op jit(solution)/shard_map/while/body/eval_jaxpr/dot_general | solution.py:43
  117.3 8.4 %fusion.85 = f32[16,16]{1,0:T(8,128)S(1)} fusion(f32[16,16,32,527]{3,2,1,0:T(8,128)S(1)} %get-tuple-element.312, f32[16,16]{1,0:T(8,128)S(1)} %get-tuple-element.313, pred[16,32,527]{2,1,0:T(8,128)(4,1)S(1)} %broadcast_and_fusion.2), kind=kLoop, calls=%fused_computation.3.clone.1 | loop fusion | flops 12951296 | bytes 17540608 | tf_op jit(solution)/shard_map/while/body/eval_jaxpr/reduce_sum | solution.py:60
  125.7 5.3 %multiply_reduce_fusion.2 = bf16[16,16,128]{2,1,0:T(8,128)(2,1)S(1)} fusion(f32[16,32,128]{2,1,0:T(8,128)S(1)} %copy.24, f32[16,16,32,527]{3,2,1,0:T(8,128)S(1)} %get-tuple-element.312, f32[16,16]{1,0:T(8,128)S(1)} %fusion.85, f32[16,16]{1,0:T(8,128)S(1)} %get-tuple-element.313, pred[16,32,527]{2,1,0:T(8,128)(4,1)S(1)} %broadcast_and_fusion.2, ...), kind=kOutput, calls=%fused_computation.5.clone.1 | convolution fusion | flops 1124532224 | bytes 21778436 | tf_op jit(solution)/shard_map/while/body/eval_jaxpr/dot_general | solution.py:61
  131.0 0.6 dynamic_slice.79
  134.4 3.3 %select_reduce_fusion.2 = (f32[16,16]{1,0:T(8,128)S(1)}, f32[16,16,32,527]{3,2,1,0:T(8,128)S(1)}) fusion(pred[16,32,527]{2,1,0:T(8,128)(4,1)S(1)} %broadcast_and_fusion.2, bf16[800,128]{1,0:T(8,128)(2,1)S(1)} %get-tuple-element.416, s32[]{:T(128)S(6)} %select_n.62, f32[16,32,128]{2,1,0:T(8,128)S(1)} %copy.25, ...), kind=kOutput, calls=%fused_computation.2.clone.1 | convolution fusion | flops 1116978944 | bytes 18125828 | tf_op jit(solution)/shard_map/while/body/eval_jaxpr/dot_general | solution.py:43
  137.7 8.4 %fusion.85 = f32[16,16]{1,0:T(8,128)S(1)} fusion(f32[16,16,32,527]{3,2,1,0:T(8,128)S(1)} %get-tuple-element.312, f32[16,16]{1,0:T(8,128)S(1)} %get-tuple-element.313, pred[16,32,527]{2,1,0:T(8,128)(4,1)S(1)} %broadcast_and_fusion.2), kind=kLoop, calls=%fused_computation.3.clone.1 | loop fusion | flops 12951296 | bytes 17540608 | tf_op jit(solution)/shard_map/while/body/eval_jaxpr/reduce_sum | solution.py:60
  146.1 5.3 %multiply_reduce_fusion.2 = bf16[16,16,128]{2,1,0:T(8,128)(2,1)S(1)} fusion(f32[16,32,128]{2,1,0:T(8,128)S(1)} %copy.24, f32[16,16,32,527]{3,2,1,0:T(8,128)S(1)} %get-tuple-element.312, f32[16,16]{1,0:T(8,128)S(1)} %fusion.85, f32[16,16]{1,0:T(8,128)S(1)} %get-tuple-element.313, pred[16,32,527]{2,1,0:T(8,128)(4,1)S(1)} %broadcast_and_fusion.2, ...), kind=kOutput, calls=%fused_computation.5.clone.1 | convolution fusion | flops 1124532224 | bytes 21778436 | tf_op jit(solution)/shard_map/while/body/eval_jaxpr/dot_general | solution.py:61
  151.4 0.6 dynamic_slice.79
  154.8 3.3 %select_reduce_fusion.2 = (f32[16,16]{1,0:T(8,128)S(1)}, f32[16,16,32,527]{3,2,1,0:T(8,128)S(1)}) fusion(pred[16,32,527]{2,1,0:T(8,128)(4,1)S(1)} %broadcast_and_fusion.2, bf16[800,128]{1,0:T(8,128)(2,1)S(1)} %get-tuple-element.416, s32[]{:T(128)S(6)} %select_n.62, f32[16,32,128]{2,1,0:T(8,128)S(1)} %copy.25, ...), kind=kOutput, calls=%fused_computation.2.clone.1 | convolution fusion | flops 1116978944 | bytes 18125828 | tf_op jit(solution)/shard_map/while/body/eval_jaxpr/dot_general | solution.py:43
  158.1 8.4 %fusion.85 = f32[16,16]{1,0:T(8,128)S(1)} fusion(f32[16,16,32,527]{3,2,1,0:T(8,128)S(1)} %get-tuple-element.312, f32[16,16]{1,0:T(8,128)S(1)} %get-tuple-element.313, pred[16,32,527]{2,1,0:T(8,128)(4,1)S(1)} %broadcast_and_fusion.2), kind=kLoop, calls=%fused_computation.3.clone.1 | loop fusion | flops 12951296 | bytes 17540608 | tf_op jit(solution)/shard_map/while/body/eval_jaxpr/reduce_sum | solution.py:60
  166.6 5.3 %multiply_reduce_fusion.2 = bf16[16,16,128]{2,1,0:T(8,128)(2,1)S(1)} fusion(f32[16,32,128]{2,1,0:T(8,128)S(1)} %copy.24, f32[16,16,32,527]{3,2,1,0:T(8,128)S(1)} %get-tuple-element.312, f32[16,16]{1,0:T(8,128)S(1)} %fusion.85, f32[16,16]{1,0:T(8,128)S(1)} %get-tuple-element.313, pred[16,32,527]{2,1,0:T(8,128)(4,1)S(1)} %broadcast_and_fusion.2, ...), kind=kOutput, calls=%fused_computation.5.clone.1 | convolution fusion | flops 1124532224 | bytes 21778436 | tf_op jit(solution)/shard_map/while/body/eval_jaxpr/dot_general | solution.py:61
  171.9 0.6 dynamic_slice.79
  175.3 3.3 %select_reduce_fusion.2 = (f32[16,16]{1,0:T(8,128)S(1)}, f32[16,16,32,527]{3,2,1,0:T(8,128)S(1)}) fusion(pred[16,32,527]{2,1,0:T(8,128)(4,1)S(1)} %broadcast_and_fusion.2, bf16[800,128]{1,0:T(8,128)(2,1)S(1)} %get-tuple-element.416, s32[]{:T(128)S(6)} %select_n.62, f32[16,32,128]{2,1,0:T(8,128)S(1)} %copy.25, ...), kind=kOutput, calls=%fused_computation.2.clone.1 | convolution fusion | flops 1116978944 | bytes 18125828 | tf_op jit(solution)/shard_map/while/body/eval_jaxpr/dot_general | solution.py:43
  178.5 8.4 %fusion.85 = f32[16,16]{1,0:T(8,128)S(1)} fusion(f32[16,16,32,527]{3,2,1,0:T(8,128)S(1)} %get-tuple-element.312, f32[16,16]{1,0:T(8,128)S(1)} %get-tuple-element.313, pred[16,32,527]{2,1,0:T(8,128)(4,1)S(1)} %broadcast_and_fusion.2), kind=kLoop, calls=%fused_computation.3.clone.1 | loop fusion | flops 12951296 | bytes 17540608 | tf_op jit(solution)/shard_map/while/body/eval_jaxpr/reduce_sum | solution.py:60
  187.0 5.3 %multiply_reduce_fusion.2 = bf16[16,16,128]{2,1,0:T(8,128)(2,1)S(1)} fusion(f32[16,32,128]{2,1,0:T(8,128)S(1)} %copy.24, f32[16,16,32,527]{3,2,1,0:T(8,128)S(1)} %get-tuple-element.312, f32[16,16]{1,0:T(8,128)S(1)} %fusion.85, f32[16,16]{1,0:T(8,128)S(1)} %get-tuple-element.313, pred[16,32,527]{2,1,0:T(8,128)(4,1)S(1)} %broadcast_and_fusion.2, ...), kind=kOutput, calls=%fused_computation.5.clone.1 | convolution fusion | flops 1124532224 | bytes 21778436 | tf_op jit(solution)/shard_map/while/body/eval_jaxpr/dot_general | solution.py:61
  192.3 0.6 dynamic_slice.79
  195.7 3.3 %select_reduce_fusion.2 = (f32[16,16]{1,0:T(8,128)S(1)}, f32[16,16,32,527]{3,2,1,0:T(8,128)S(1)}) fusion(pred[16,32,527]{2,1,0:T(8,128)(4,1)S(1)} %broadcast_and_fusion.2, bf16[800,128]{1,0:T(8,128)(2,1)S(1)} %get-tuple-element.416, s32[]{:T(128)S(6)} %select_n.62, f32[16,32,128]{2,1,0:T(8,128)S(1)} %copy.25, ...), kind=kOutput, calls=%fused_computation.2.clone.1 | convolution fusion | flops 1116978944 | bytes 18125828 | tf_op jit(solution)/shard_map/while/body/eval_jaxpr/dot_general | solution.py:43
  198.9 8.4 %fusion.85 = f32[16,16]{1,0:T(8,128)S(1)} fusion(f32[16,16,32,527]{3,2,1,0:T(8,128)S(1)} %get-tuple-element.312, f32[16,16]{1,0:T(8,128)S(1)} %get-tuple-element.313, pred[16,32,527]{2,1,0:T(8,128)(4,1)S(1)} %broadcast_and_fusion.2), kind=kLoop, calls=%fused_computation.3.clone.1 | loop fusion | flops 12951296 | bytes 17540608 | tf_op jit(solution)/shard_map/while/body/eval_jaxpr/reduce_sum | solution.py:60
  207.4 5.3 %multiply_reduce_fusion.2 = bf16[16,16,128]{2,1,0:T(8,128)(2,1)S(1)} fusion(f32[16,32,128]{2,1,0:T(8,128)S(1)} %copy.24, f32[16,16,32,527]{3,2,1,0:T(8,128)S(1)} %get-tuple-element.312, f32[16,16]{1,0:T(8,128)S(1)} %fusion.85, f32[16,16]{1,0:T(8,128)S(1)} %get-tuple-element.313, pred[16,32,527]{2,1,0:T(8,128)(4,1)S(1)} %broadcast_and_fusion.2, ...), kind=kOutput, calls=%fused_computation.5.clone.1 | convolution fusion | flops 1124532224 | bytes 21778436 | tf_op jit(solution)/shard_map/while/body/eval_jaxpr/dot_general | solution.py:61
  216.1 3.3 %select_reduce_fusion.2 = (f32[16,16]{1,0:T(8,128)S(1)}, f32[16,16,32,527]{3,2,1,0:T(8,128)S(1)}) fusion(pred[16,32,527]{2,1,0:T(8,128)(4,1)S(1)} %broadcast_and_fusion.2, bf16[800,128]{1,0:T(8,128)(2,1)S(1)} %get-tuple-element.416, s32[]{:T(128)S(6)} %select_n.62, f32[16,32,128]{2,1,0:T(8,128)S(1)} %copy.25, ...), kind=kOutput, calls=%fused_computation.2.clone.1 | convolution fusion | flops 1116978944 | bytes 18125828 | tf_op jit(solution)/shard_map/while/body/eval_jaxpr/dot_general | solution.py:43
  219.4 8.4 %fusion.85 = f32[16,16]{1,0:T(8,128)S(1)} fusion(f32[16,16,32,527]{3,2,1,0:T(8,128)S(1)} %get-tuple-element.312, f32[16,16]{1,0:T(8,128)S(1)} %get-tuple-element.313, pred[16,32,527]{2,1,0:T(8,128)(4,1)S(1)} %broadcast_and_fusion.2), kind=kLoop, calls=%fused_computation.3.clone.1 | loop fusion | flops 12951296 | bytes 17540608 | tf_op jit(solution)/shard_map/while/body/eval_jaxpr/reduce_sum | solution.py:60
  227.8 5.3 %multiply_reduce_fusion.2 = bf16[16,16,128]{2,1,0:T(8,128)(2,1)S(1)} fusion(f32[16,32,128]{2,1,0:T(8,128)S(1)} %copy.24, f32[16,16,32,527]{3,2,1,0:T(8,128)S(1)} %get-tuple-element.312, f32[16,16]{1,0:T(8,128)S(1)} %fusion.85, f32[16,16]{1,0:T(8,128)S(1)} %get-tuple-element.313, pred[16,32,527]{2,1,0:T(8,128)(4,1)S(1)} %broadcast_and_fusion.2, ...), kind=kOutput, calls=%fused_computation.5.clone.1 | convolution fusion | flops 1124532224 | bytes 21778436 | tf_op jit(solution)/shard_map/while/body/eval_jaxpr/dot_general | solution.py:61
  233.1 0.6 dynamic_slice.79
  236.5 3.3 %select_reduce_fusion.2 = (f32[16,16]{1,0:T(8,128)S(1)}, f32[16,16,32,527]{3,2,1,0:T(8,128)S(1)}) fusion(pred[16,32,527]{2,1,0:T(8,128)(4,1)S(1)} %broadcast_and_fusion.2, bf16[800,128]{1,0:T(8,128)(2,1)S(1)} %get-tuple-element.416, s32[]{:T(128)S(6)} %select_n.62, f32[16,32,128]{2,1,0:T(8,128)S(1)} %copy.25, ...), kind=kOutput, calls=%fused_computation.2.clone.1 | convolution fusion | flops 1116978944 | bytes 18125828 | tf_op jit(solution)/shard_map/while/body/eval_jaxpr/dot_general | solution.py:43
  239.8 8.4 %fusion.85 = f32[16,16]{1,0:T(8,128)S(1)} fusion(f32[16,16,32,527]{3,2,1,0:T(8,128)S(1)} %get-tuple-element.312, f32[16,16]{1,0:T(8,128)S(1)} %get-tuple-element.313, pred[16,32,527]{2,1,0:T(8,128)(4,1)S(1)} %broadcast_and_fusion.2), kind=kLoop, calls=%fused_computation.3.clone.1 | loop fusion | flops 12951296 | bytes 17540608 | tf_op jit(solution)/shard_map/while/body/eval_jaxpr/reduce_sum | solution.py:60
  248.2 5.3 %multiply_reduce_fusion.2 = bf16[16,16,128]{2,1,0:T(8,128)(2,1)S(1)} fusion(f32[16,32,128]{2,1,0:T(8,128)S(1)} %copy.24, f32[16,16,32,527]{3,2,1,0:T(8,128)S(1)} %get-tuple-element.312, f32[16,16]{1,0:T(8,128)S(1)} %fusion.85, f32[16,16]{1,0:T(8,128)S(1)} %get-tuple-element.313, pred[16,32,527]{2,1,0:T(8,128)(4,1)S(1)} %broadcast_and_fusion.2, ...), kind=kOutput, calls=%fused_computation.5.clone.1 | convolution fusion | flops 1124532224 | bytes 21778436 | tf_op jit(solution)/shard_map/while/body/eval_jaxpr/dot_general | solution.py:61
  253.5 0.6 dynamic_slice.79
  256.9 3.3 %select_reduce_fusion.2 = (f32[16,16]{1,0:T(8,128)S(1)}, f32[16,16,32,527]{3,2,1,0:T(8,128)S(1)}) fusion(pred[16,32,527]{2,1,0:T(8,128)(4,1)S(1)} %broadcast_and_fusion.2, bf16[800,128]{1,0:T(8,128)(2,1)S(1)} %get-tuple-element.416, s32[]{:T(128)S(6)} %select_n.62, f32[16,32,128]{2,1,0:T(8,128)S(1)} %copy.25, ...), kind=kOutput, calls=%fused_computation.2.clone.1 | convolution fusion | flops 1116978944 | bytes 18125828 | tf_op jit(solution)/shard_map/while/body/eval_jaxpr/dot_general | solution.py:43
  260.2 8.4 %fusion.85 = f32[16,16]{1,0:T(8,128)S(1)} fusion(f32[16,16,32,527]{3,2,1,0:T(8,128)S(1)} %get-tuple-element.312, f32[16,16]{1,0:T(8,128)S(1)} %get-tuple-element.313, pred[16,32,527]{2,1,0:T(8,128)(4,1)S(1)} %broadcast_and_fusion.2), kind=kLoop, calls=%fused_computation.3.clone.1 | loop fusion | flops 12951296 | bytes 17540608 | tf_op jit(solution)/shard_map/while/body/eval_jaxpr/reduce_sum | solution.py:60
  268.7 5.3 %multiply_reduce_fusion.2 = bf16[16,16,128]{2,1,0:T(8,128)(2,1)S(1)} fusion(f32[16,32,128]{2,1,0:T(8,128)S(1)} %copy.24, f32[16,16,32,527]{3,2,1,0:T(8,128)S(1)} %get-tuple-element.312, f32[16,16]{1,0:T(8,128)S(1)} %fusion.85, f32[16,16]{1,0:T(8,128)S(1)} %get-tuple-element.313, pred[16,32,527]{2,1,0:T(8,128)(4,1)S(1)} %broadcast_and_fusion.2, ...), kind=kOutput, calls=%fused_computation.5.clone.1 | convolution fusion | flops 1124532224 | bytes 21778436 | tf_op jit(solution)/shard_map/while/body/eval_jaxpr/dot_general | solution.py:61
  274.0 0.6 dynamic_slice.79
  277.4 3.3 %select_reduce_fusion.2 = (f32[16,16]{1,0:T(8,128)S(1)}, f32[16,16,32,527]{3,2,1,0:T(8,128)S(1)}) fusion(pred[16,32,527]{2,1,0:T(8,128)(4,1)S(1)} %broadcast_and_fusion.2, bf16[800,128]{1,0:T(8,128)(2,1)S(1)} %get-tuple-element.416, s32[]{:T(128)S(6)} %select_n.62, f32[16,32,128]{2,1,0:T(8,128)S(1)} %copy.25, ...), kind=kOutput, calls=%fused_computation.2.clone.1 | convolution fusion | flops 1116978944 | bytes 18125828 | tf_op jit(solution)/shard_map/while/body/eval_jaxpr/dot_general | solution.py:43
  280.6 8.4 %fusion.85 = f32[16,16]{1,0:T(8,128)S(1)} fusion(f32[16,16,32,527]{3,2,1,0:T(8,128)S(1)} %get-tuple-element.312, f32[16,16]{1,0:T(8,128)S(1)} %get-tuple-element.313, pred[16,32,527]{2,1,0:T(8,128)(4,1)S(1)} %broadcast_and_fusion.2), kind=kLoop, calls=%fused_computation.3.clone.1 | loop fusion | flops 12951296 | bytes 17540608 | tf_op jit(solution)/shard_map/while/body/eval_jaxpr/reduce_sum | solution.py:60
  289.1 5.3 %multiply_reduce_fusion.2 = bf16[16,16,128]{2,1,0:T(8,128)(2,1)S(1)} fusion(f32[16,32,128]{2,1,0:T(8,128)S(1)} %copy.24, f32[16,16,32,527]{3,2,1,0:T(8,128)S(1)} %get-tuple-element.312, f32[16,16]{1,0:T(8,128)S(1)} %fusion.85, f32[16,16]{1,0:T(8,128)S(1)} %get-tuple-element.313, pred[16,32,527]{2,1,0:T(8,128)(4,1)S(1)} %broadcast_and_fusion.2, ...), kind=kOutput, calls=%fused_computation.5.clone.1 | convolution fusion | flops 1124532224 | bytes 21778436 | tf_op jit(solution)/shard_map/while/body/eval_jaxpr/dot_general | solution.py:61
  294.4 15.9 %all_to_all.30 = bf16[160,1,16,128]{3,2,1,0:T(8,128)(2,1)S(1)} all-to-all(bf16[160,1,16,128]{3,2,1,0:T(8,128)(2,1)S(1)} %bitcast.450), channel_id=1, replica_groups=mesh['seq'=8,'head'=4] {'head'}, dimensions={0} | all-to-all | bytes 1310720 | tf_op jit(solution)/shard_map/all_to_all | solution.py:124
  310.3 1.0 copy.19
  (750 shorter events, 20.6 us)
Async XLA Ops:
  0.0 16.2 %collective-permute-start = (bf16[40,128]{1,0:T(8,128)(2,1)}, bf16[40,128]{1,0:T(8,128)(2,1)S(1)}, u32[]{:S(2)}, u32[]{:S(2)}) collective-permute-start(bf16[40,128]{1,0:T(8,128)(2,1)} %param.10), channel_id=1, source_target_pairs={{0,4},{4,8},{8,12},{12,16},{16,20},{20,24},{24,28},{1,5},{5,9},{9,... | collective-permute-start | bytes 30728 | tf_op jit(solution)/shard_map/ppermute | solution.py:15
  1.9 15.0 %collective-permute-start.1 = (bf16[40,128]{1,0:T(8,128)(2,1)}, bf16[40,128]{1,0:T(8,128)(2,1)S(1)}, u32[]{:S(2)}, u32[]{:S(2)}) collective-permute-start(bf16[40,128]{1,0:T(8,128)(2,1)} %param.8), channel_id=1, source_target_pairs={{0,4},{4,8},{8,12},{12,16},{16,20},{20,24},{24,28},{1,5},{5,9},{9,... | collective-permute-start | bytes 30728 | tf_op jit(solution)/shard_map/ppermute | solution.py:15
  5.4 15.6 %collective-permute-start.5 = (bf16[40,128]{1,0:T(8,128)(2,1)}, bf16[40,128]{1,0:T(8,128)(2,1)S(1)}, u32[]{:S(2)}, u32[]{:S(2)}) collective-permute-start(bf16[40,128]{1,0:T(8,128)(2,1)} %param.9), channel_id=1, source_target_pairs={{0,4},{4,8},{8,12},{12,16},{16,20},{20,24},{24,28},{1,5},{5,9},{9,... | collective-permute-start | bytes 30728 | tf_op jit(solution)/shard_map/ppermute | solution.py:15
  9.4 80.8 %all-to-all-start = ((bf16[40,4,16,128]{3,2,0,1:T(8,128)(2,1)}), bf16[40,4,16,128]{3,2,0,1:T(8,128)(2,1)S(1)}, u32[]{:S(2)}, u32[]{:S(2)}) async-start(bf16[40,4,16,128]{3,2,0,1:T(8,128)(2,1)} %copy.18), calls=%async_computation | async-start | bytes 1310720 | tf_op jit(solution)/shard_map/all_to_all | solution.py:103
  14.3 6.1 %collective-permute-start.9 = (bf16[40,128]{1,0:T(8,128)(2,1)}, bf16[40,128]{1,0:T(8,128)(2,1)S(1)}, u32[]{:S(2)}, u32[]{:S(2)}) collective-permute-start(bf16[40,128]{1,0:T(8,128)(2,1)} %param.11), channel_id=1, source_target_pairs={{0,4},{4,8},{8,12},{12,16},{16,20},{20,24},{24,28},{1,5},{5,9},{9,... | collective-permute-start | bytes 30728 | tf_op jit(solution)/shard_map/ppermute | solution.py:15
  16.9 6.1 %collective-permute-start.2 = (bf16[40,128]{1,0:T(8,128)(2,1)S(1)}, bf16[40,128]{1,0:T(8,128)(2,1)S(1)}, u32[]{:S(2)}, u32[]{:S(2)}) collective-permute-start(bf16[40,128]{1,0:T(8,128)(2,1)S(1)} %collective-permute-done.1), channel_id=1, source_target_pairs={{0,4},{4,8},{8,12},{12,16},{16,20},{20,24},{24,28},{1,5},{5,9},{9,... | collective-permute-start | bytes 30728 | tf_op jit(solution)/shard_map/ppermute | solution.py:15
  21.1 17.7 %collective-permute-start.6 = (bf16[40,128]{1,0:T(8,128)(2,1)S(1)}, bf16[40,128]{1,0:T(8,128)(2,1)S(1)}, u32[]{:S(2)}, u32[]{:S(2)}) collective-permute-start(bf16[40,128]{1,0:T(8,128)(2,1)S(1)} %collective-permute-done.5), channel_id=1, source_target_pairs={{0,4},{4,8},{8,12},{12,16},{16,20},{20,24},{24,28},{1,5},{5,9},{9,... | collective-permute-start | bytes 30728 | tf_op jit(solution)/shard_map/ppermute | solution.py:15
  23.0 17.7 %collective-permute-start.3 = (bf16[40,128]{1,0:T(8,128)(2,1)S(1)}, bf16[40,128]{1,0:T(8,128)(2,1)S(1)}, u32[]{:S(2)}, u32[]{:S(2)}) collective-permute-start(bf16[40,128]{1,0:T(8,128)(2,1)S(1)} %collective-permute-done.2), channel_id=1, source_target_pairs={{0,4},{4,8},{8,12},{12,16},{16,20},{20,24},{24,28},{1,5},{5,9},{9,... | collective-permute-start | bytes 30728 | tf_op jit(solution)/shard_map/ppermute | solution.py:15
  38.8 17.1 %collective-permute-start.7 = (bf16[40,128]{1,0:T(8,128)(2,1)S(1)}, bf16[40,128]{1,0:T(8,128)(2,1)S(1)}, u32[]{:S(2)}, u32[]{:S(2)}) collective-permute-start(bf16[40,128]{1,0:T(8,128)(2,1)S(1)} %collective-permute-done.6), channel_id=1, source_target_pairs={{0,4},{4,8},{8,12},{12,16},{16,20},{20,24},{24,28},{1,5},{5,9},{9,... | collective-permute-start | bytes 30728 | tf_op jit(solution)/shard_map/ppermute | solution.py:15
  40.7 17.1 %collective-permute-start.4 = (bf16[40,128]{1,0:T(8,128)(2,1)S(1)}, bf16[40,128]{1,0:T(8,128)(2,1)S(1)}, u32[]{:S(2)}, u32[]{:S(2)}) collective-permute-start(bf16[40,128]{1,0:T(8,128)(2,1)S(1)} %collective-permute-done.3), channel_id=1, source_target_pairs={{0,4},{4,8},{8,12},{12,16},{16,20},{20,24},{24,28},{1,5},{5,9},{9,... | collective-permute-start | bytes 30728 | tf_op jit(solution)/shard_map/ppermute | solution.py:15
  55.9 5.9 %collective-permute-start.8 = (bf16[40,128]{1,0:T(8,128)(2,1)S(1)}, bf16[40,128]{1,0:T(8,128)(2,1)S(1)}, u32[]{:S(2)}, u32[]{:S(2)}) collective-permute-start(bf16[40,128]{1,0:T(8,128)(2,1)S(1)} %collective-permute-done.7), channel_id=1, source_target_pairs={{0,4},{4,8},{8,12},{12,16},{16,20},{20,24},{24,28},{1,5},{5,9},{9,... | collective-permute-start | bytes 30728 | tf_op jit(solution)/shard_map/ppermute | solution.py:15
where the time goes:
time: 314 us; the launch traced here: 311 us
  other arithmetic  89.6 us (29%)
  matrix products  85.2 us (27%)
  blocking collectives  70.7 us (23%)
  local copies, waits for them, and re-layouts  26.2 us (8%)
  starting transfers between devices  25.6 us (8%)
  loops' own time  9.12 us (3%)
  waiting for transfers between devices  4.73 us (2%)
    reduce_sum x10, other arithmetic, window_attend(): jnp.sum(raised, axis=(2, 3), keepdims=True)  84.1 us
    dot_general x10, matrix products, window_attend(): jnp.dot(weights.reshape(-1, key_span), values_one, preferred_element_type...  52.6 us
    dot_general x10, matrix products, window_attend(): lax.dot_general(product.reshape(-1, head_depth), keys_one, (((1,), (1,)),...  32.6 us
    ppermute x10, starting transfers between devices, from_behind(): return lax.ppermute(shard, axis, pairs)  20.7 us
    all_to_all x1, blocking collectives, body(): lax.all_to_all(result, 'head', split_axis=0, concat_axis=1, tiled=True)  15.9 us
    while x620, local copies, waits for them, and re-layouts  14.8 us
    all_gather x1, blocking collectives, body(): lax.all_gather(stack_keys_one, 'head', axis=1, tiled=True)  14.1 us
    all_gather x1, blocking collectives, body(): lax.all_gather(stack_keys_two, 'head', axis=1, tiled=True)  13.9 us
  transfers between devices with their start and end apart: 11, of which 2 were waited for; matrix products, arithmetic and copies ran while one was open for 2% of the time, Pallas kernels for 0%

commit v1 on v0

v1 whole, which is shorter than its diff:
```python
import functools
import math

import jax
import jax.numpy as jnp
from jax import lax
from jax.experimental import pallas as pl
from jax.experimental.pallas import tpu as pltpu
from jax.sharding import PartitionSpec as P

WIN_ONE = 512
WIN_TWO = 32
LAG_CHUNK = 8


def pieces_behind(window, rows):
    return (window - 2) // rows + 1


def halo_kernel(reach, k1, v1, k2, v2, k1_out, v1_out, k2_out, v2_out, send, recv):
    inner = lax.axis_size("head")
    count = lax.axis_size("seq") * inner
    me = lax.axis_index("seq") * inner + lax.axis_index("head")
    flows = [(k1, k1_out, reach[0]), (v1, v1_out, reach[0])]
    flows += [(k2, k2_out, reach[1]), (v2, v2_out, reach[1])]
    far = max(reach)

    def place(index):
        return (index // inner, index % inner)

    barrier = pltpu.get_barrier_semaphore()
    for step in range(1, far + 1):

        @pl.when(me - step >= 0)
        def _():
            pl.semaphore_signal(
                barrier, inc=1, device_id=place(me - step), device_id_type=pl.DeviceIdType.MESH
            )

    @pl.when(me + 1 < count)
    def _():
        pl.semaphore_wait(barrier, jnp.minimum(far, count - 1 - me))

    def copies(step):
        made = []
        for flow, (source, target, width) in enumerate(flows):
            if step <= width:
                made.append(
                    pltpu.make_async_remote_copy(
                        src_ref=source,
                        dst_ref=target.at[width - step],
                        send_sem=send.at[flow, step - 1],
                        recv_sem=recv.at[flow, step - 1],
                        device_id=place(me + step),
                        device_id_type=pl.DeviceIdType.MESH,
                    )
                )
        return made

    for step in range(far, 0, -1):

        @pl.when(me + step < count)
        def _():
            for copy in copies(step):
                copy.start()

    for step in range(far, 0, -1):

        @pl.when(me + step < count)
        def _():
            for copy in copies(step):
                copy.wait_send()

        @pl.when(me - step >= 0)
        def _():
            for copy in copies(step):
                copy.wait_recv()


def attend_kernel(
    q, k1h, v1h, k2h, v2h, k1, v1, k2, v2, out, k1f, v1f, k2f, v2f, one2, kw, vw, s_first
):
    piece, heads, depth = q.shape
    inner = lax.axis_size("head")
    me = lax.axis_index("seq") * inner + lax.axis_index("head")
    lead_one = k1h.shape[0] * piece
    lead_two = k2h.shape[0] * piece
    scale = 1.0 / math.sqrt(depth)

    def spread(target, behind, own):
        for slot in range(behind.shape[0]):
            target[slot * piece : (slot + 1) * piece, :] = behind[slot].astype(jnp.float32)
        lead = behind.shape[0] * piece
        target[lead : lead + piece, :] = own[...].astype(jnp.float32)

    spread(k1f, k1h, k1)
    spread(v1f, v1h, v1)
    spread(k2f, k2h, k2)
    spread(v2f, v2h, v2)
    first_one = lead_one - me * piece
    first_two = lead_two - me * piece

    @pl.when(first_one > 0)
    def _():
        pos = lax.broadcasted_iota(jnp.int32, k1f.shape, 0)
        whole = k1f[...]
        head_row = jnp.sum(jnp.where(pos == first_one, whole, 0.0), axis=0, keepdims=True)
        k1f[...] = jnp.where(pos < first_one, head_row, whole)
        v1f[...] = jnp.where(pos < first_one, 0.0, v1f[...])

    pos_two = lax.broadcasted_iota(jnp.int32, k2f.shape, 0)
    whole_two = k2f[...]
    head_two = jnp.sum(jnp.where(pos_two == first_two, whole_two, 0.0), axis=0, keepdims=True)
    k2f[...] = jnp.where(pos_two < first_two, head_two, whole_two) * scale
    v2f[...] = jnp.where(pos_two < first_two, 0.0, v2f[...])
    one2[...] = jnp.where(pos_two < first_two, 0.0, 1.0)

    def load_keys(token):
        kw[...] = k1f[pl.ds(lead_one + token - (WIN_ONE - 1), WIN_ONE), :].astype(jnp.bfloat16)

    def logits(token, chunk):
        query = q[token].astype(jnp.float32)
        rows = []
        for lag in range(chunk * LAG_CHUNK, (chunk + 1) * LAG_CHUNK):
            near = k2f[pl.ds(lead_two + token - lag, 1), :]
            rows.append((query * near).astype(jnp.bfloat16))
        return lax.dot_general(
            jnp.concatenate(rows, axis=0),
            kw[...],
            (((1,), (1,)), ((), ())),
            preferred_element_type=jnp.float32,
        )

    load_keys(0)
    s_first[...] = logits(0, 0)
    lane_pos = lax.broadcasted_iota(jnp.int32, (WIN_ONE, depth), 0)

    def step(token, carry):
        start = lead_one + token - (WIN_ONE - 1)
        vw[:, :depth] = v1f[pl.ds(start, WIN_ONE), :].astype(jnp.bfloat16)
        vw[:, depth:] = jnp.where(lane_pos + start < first_one, 0.0, 1.0).astype(jnp.bfloat16)
        peak = num = den = None
        chunks = WIN_TWO // LAG_CHUNK
        scores = s_first[...]
        for chunk in range(chunks):
            if chunk + 1 < chunks:
                following = logits(token, chunk + 1)
            else:
                later = jnp.minimum(token + 1, piece - 1)
                load_keys(later)
                s_first[...] = logits(later, 0)
            parts = scores.reshape(LAG_CHUNK, heads, WIN_ONE)
            top = jnp.max(jnp.max(parts, axis=0), axis=1, keepdims=True)
            raised_peak = top if peak is None else jnp.maximum(peak, top)
            raised = jnp.exp(parts - raised_peak[None]).astype(jnp.bfloat16)
            mixed = jnp.dot(
                raised.reshape(LAG_CHUNK * heads, WIN_ONE), vw[...], preferred_element_type=jnp.float32
            )
            mixed = mixed.reshape(LAG_CHUNK, heads, 2 * depth)
            if peak is not None:
                fade = jnp.exp(peak - raised_peak)
                num = num * fade
                den = den * fade
            for index in range(LAG_CHUNK):
                row = lead_two + token - (chunk * LAG_CHUNK + index)
                more = mixed[index, :, :depth] * v2f[pl.ds(row, 1), :]
                count = mixed[index, :, depth:] * one2[pl.ds(row, 1), :]
                num = more if num is None else num + more
                den = count if den is None else den + count
            peak = raised_peak
            if chunk + 1 < chunks:
                scores = following
        out[token] = (num / den).astype(out.dtype)
        return carry

    lax.fori_loop(0, piece, step, 0)


def body(queries, key_one, value_one, key_two, value_two):
    piece, heads, depth = queries.shape
    reach = (pieces_behind(WIN_ONE, piece), pieces_behind(WIN_TWO, piece))
    anywhere = pl.BlockSpec(memory_space=pl.ANY)
    vmem = pl.BlockSpec(memory_space=pltpu.VMEM)
    behind = [jax.ShapeDtypeStruct((r, piece, depth), key_one.dtype) for r in (reach[0], reach[0], reach[1], reach[1])]
    halos = pl.pallas_call(
        functools.partial(halo_kernel, reach),
        out_shape=behind,
        in_specs=[anywhere] * 4,
        out_specs=[anywhere] * 4,
        scratch_shapes=[
            pltpu.SemaphoreType.DMA((4, max(reach))),
            pltpu.SemaphoreType.DMA((4, max(reach))),
        ],
        compiler_params=pltpu.CompilerParams(collective_id=0, has_side_effects=True),
    )(key_one, value_one, key_two, value_two)
    long_one = ((reach[0] + 1) * piece, depth)
    long_two = ((reach[1] + 1) * piece, depth)
    return pl.pallas_call(
        attend_kernel,
        out_shape=jax.ShapeDtypeStruct(queries.shape, queries.dtype),
        in_specs=[vmem] * 9,
        out_specs=vmem,
        scratch_shapes=[
            pltpu.VMEM(long_one, jnp.float32),
            pltpu.VMEM(long_one, jnp.float32),
            pltpu.VMEM(long_two, jnp.float32),
            pltpu.VMEM(long_two, jnp.float32),
            pltpu.VMEM(long_two, jnp.float32),
            pltpu.VMEM((WIN_ONE, depth), jnp.bfloat16),
            pltpu.VMEM((WIN_ONE, 2 * depth), jnp.bfloat16),
            pltpu.VMEM((LAG_CHUNK * heads, WIN_ONE), jnp.float32),
        ],
        compiler_params=pltpu.CompilerParams(vmem_limit_bytes=48 * 1024 * 1024),
    )(queries, *halos, key_one, value_one, key_two, value_two)


def solution(mesh):
    rows = P(("seq", "head"), None)
    placed = (P(("seq", "head"), None, None), rows, rows, rows, rows)
    return jax.shard_map(
        body, mesh=mesh, in_specs=placed, out_specs=P(("seq", "head"), None, None), check_vma=False
    )
```

time: 314 us -> 94 us (0.30)
  other arithmetic: 89.6 us -> 0 us
  Pallas kernels: 0 us -> 89.1 us
  matrix products: 85.2 us -> 0 us
  blocking collectives: 70.7 us -> 0 us
  starting transfers between devices: 25.6 us -> 0 us
  local copies, waits for them, and re-layouts: 26.2 us -> 4.31 us
  loops' own time: 9.12 us -> 0 us
  waiting for transfers between devices: 4.73 us -> 0 us
    pallas_call x0 -> x2, Pallas kernels: none -> 89.1 us  [the longest x1 74.7 us: body(): pl.pallas_call(attend_kernel, out_shape=jax.ShapeDtypeStruct(queries.shap...]
    dot_general x20 -> x0, matrix products: 85.2 us -> none  [the longest x10 52.6 us: window_attend(): jnp.dot(weights.reshape(-1, key_span), values_one, preferred_element_type...]
    reduce_sum x10 -> x0, other arithmetic: 84.1 us -> none  [window_attend(): jnp.sum(raised, axis=(2, 3), keepdims=True)]
    all_gather x4 -> x0, blocking collectives: 54.7 us -> none  [the longest x1 14.1 us: body(): lax.all_gather(stack_keys_one, 'head', axis=1, tiled=True)]
    ppermute x10 -> x0, starting transfers between devices: 20.7 us -> none  [from_behind(): return lax.ppermute(shard, axis, pairs)]
    all_to_all x1 -> x0, blocking collectives: 15.9 us -> none  [body(): lax.all_to_all(result, 'head', split_axis=0, concat_axis=1, tiled=True)]
    while x620 -> x0, local copies, waits for them, and re-layouts: 14.8 us -> none
    another operation x1 -> x0, loops' own time: 9.12 us -> none  [body(): lax.map(attend, jnp.arange(row_count // block_rows, dtype=jnp.int32))]
  transfers between devices with their start and end apart: 11 -> 0, of which waited for: 2 -> 0; matrix products, arithmetic and copies ran while one was open for 2% -> 0% of each run, Pallas kernels for 0% -> 0%
where the time goes in v1:
time: 94 us; the launch traced here: 93.5 us
  Pallas kernels  89.1 us (95%)
  local copies, waits for them, and re-layouts  4.31 us (5%)
    pallas_call x1, Pallas kernels, body(): pl.pallas_call(attend_kernel, out_shape=jax.ShapeDtypeStruct(queries.shap...  74.7 us
    pallas_call x1, Pallas kernels, body(): pl.pallas_call(functools.partial(halo_kernel, reach), out_shape=behind, i...  14.4 us
    unnamed x18, local copies, waits for them, and re-layouts  4.31 us

profile of v1, /device:TPU:4, one launch (start us, length us, event | category | flops | bytes accessed | tf_op | source)
XLA Modules:
  0.0 93.5 jit_solution(5295105629699462196)
XLA Ops:
  0.0 0.0 copy-start.3
  0.0 0.0 copy-start.4
  0.0 0.0 copy-start.5
  0.0 0.0 copy-start.6
  0.0 14.4 %shard_map.55 = (bf16[13,40,128]{2,1,0:T(8,128)(2,1)}, bf16[13,40,128]{2,1,0:T(8,128)(2,1)}, bf16[1,40,128]{2,1,0:T(8,128)(2,1)}, bf16[1,40,128]{2,1,0:T(8,128)(2,1)}) custom-call(bf16[40,128]{1,0:T(8,128)(2,1)} %k1.3, bf16[40,128]{1,0:T(8,128)(2,1)} %v1.3, bf16[40,128]{1,0:T(8,128)(2,1)} %k2.3, bf16[40,128]{1,0:T(8,128)(2,1)} %v2.3), custom_call_target="tpu_custom_call" | custom-call | tf_op jit(solution)/shard_map/pallas_call | solution.py:185
  14.4 0.0 copy-done.3
  14.4 0.0 copy-done.4
  14.4 0.0 copy-done.5
  14.4 0.0 copy-done.6
  14.4 0.0 copy-start
  14.4 1.1 %copy-done = bf16[40,64,128]{2,1,0:T(8,128)(2,1)S(1)} copy-done((bf16[40,64,128]{2,1,0:T(8,128)(2,1)S(1)}, bf16[40,64,128]{2,1,0:T(8,128)(2,1)}, u32[]{:S(2)}) %copy-start) | copy-done | bytes 655384
  15.5 0.0 copy-start.1
  15.5 0.9 copy-done.1
  16.4 0.0 copy-start.2
  16.4 0.9 copy-done.2
  17.3 0.0 copy-start.7
  17.3 0.7 copy-done.7
  18.0 0.0 copy-start.8
  18.0 0.7 copy-done.8
  18.7 74.7 %shard_map.56 = bf16[40,64,128]{2,1,0:T(8,128)(2,1)} custom-call(bf16[40,64,128]{2,1,0:T(8,128)(2,1)S(1)} %copy-done, bf16[13,40,128]{2,1,0:T(8,128)(2,1)S(1)} %copy-done.1, bf16[13,40,128]{2,1,0:T(8,128)(2,1)S(1)} %copy-done.2, bf16[1,40,128]{2,1,0:T(8,128)(2,1)S(1)} %copy-done.7, bf16[1,40,128]{2,1,0:T(8,128)(2,1)S(1)} %copy-done.8, ...), custom_call_target="tpu_custom_call" | custom-call | tf_op jit(solution)/shard_map/pallas_call | solution.py:198
Async XLA Ops:
  0.0 14.4 %copy-start.3 = (bf16[40,128]{1,0:T(8,128)(2,1)S(1)}, bf16[40,128]{1,0:T(8,128)(2,1)}, u32[]{:S(2)}) copy-start(bf16[40,128]{1,0:T(8,128)(2,1)} %k1.3) | copy-start | bytes 30724
  0.0 14.4 %copy-start.4 = (bf16[40,128]{1,0:T(8,128)(2,1)S(1)}, bf16[40,128]{1,0:T(8,128)(2,1)}, u32[]{:S(2)}) copy-start(bf16[40,128]{1,0:T(8,128)(2,1)} %v1.3) | copy-start | bytes 30724
  0.0 14.4 %copy-start.5 = (bf16[40,128]{1,0:T(8,128)(2,1)S(1)}, bf16[40,128]{1,0:T(8,128)(2,1)}, u32[]{:S(2)}) copy-start(bf16[40,128]{1,0:T(8,128)(2,1)} %k2.3) | copy-start | bytes 30724
  0.0 14.4 %copy-start.6 = (bf16[40,128]{1,0:T(8,128)(2,1)S(1)}, bf16[40,128]{1,0:T(8,128)(2,1)}, u32[]{:S(2)}) copy-start(bf16[40,128]{1,0:T(8,128)(2,1)} %v2.3) | copy-start | bytes 30724
  14.4 1.1 %copy-start = (bf16[40,64,128]{2,1,0:T(8,128)(2,1)S(1)}, bf16[40,64,128]{2,1,0:T(8,128)(2,1)}, u32[]{:S(2)}) copy-start(bf16[40,64,128]{2,1,0:T(8,128)(2,1)} %q.1) | copy-start | bytes 1966084
  15.5 0.9 copy-start.1
  16.4 0.9 copy-start.2
  17.3 0.7 copy-start.7
  18.0 0.7 copy-start.8

commit v2 on v1

--- a/solution.py
+++ b/solution.py
@@ -11,6 +11,9 @@
 WIN_ONE = 512
 WIN_TWO = 32
 LAG_CHUNK = 8
+ROW_L = 1
+COL_L = 2
+ROW_B = 2
 
 
 def pieces_behind(window, rows):
@@ -78,7 +81,7 @@
 
 
 def attend_kernel(
-    q, k1h, v1h, k2h, v2h, k1, v1, k2, v2, out, k1f, v1f, k2f, v2f, one2, kw, vw, s_first
+    q, k1h, v1h, k2h, v2h, k1, v1, k2, v2, out, k1f, v1f, k2f, v2f, one2, kw, vw, scores
 ):
     piece, heads, depth = q.shape
     inner = lax.axis_size("head")
@@ -115,65 +118,69 @@
     v2f[...] = jnp.where(pos_two < first_two, 0.0, v2f[...])
     one2[...] = jnp.where(pos_two < first_two, 0.0, 1.0)
 
+    span = LAG_CHUNK * heads
+    lane_pos = lax.broadcasted_iota(jnp.int32, (WIN_ONE, depth), 0)
+
     def load_keys(token):
         kw[...] = k1f[pl.ds(lead_one + token - (WIN_ONE - 1), WIN_ONE), :].astype(jnp.bfloat16)
 
-    def logits(token, chunk):
+    def logits(token, chunk, top):
         query = q[token].astype(jnp.float32)
         rows = []
         for lag in range(chunk * LAG_CHUNK, (chunk + 1) * LAG_CHUNK):
             near = k2f[pl.ds(lead_two + token - lag, 1), :]
             rows.append((query * near).astype(jnp.bfloat16))
-        return lax.dot_general(
-            jnp.concatenate(rows, axis=0),
-            kw[...],
-            (((1,), (1,)), ((), ())),
-            preferred_element_type=jnp.float32,
-        )
-
+        product = jnp.concatenate(rows, axis=0)
+        for lo in range(0, span, span // ROW_L):
+            for col in range(0, WIN_ONE, WIN_ONE // COL_L):
+                made = lax.dot_general(
+                    product[lo : lo + span // ROW_L],
+                    kw[col : col + WIN_ONE // COL_L, :],
+                    (((1,), (1,)), ((), ())),
+                    preferred_element_type=jnp.float32,
+                )
+                scores[chunk * span + lo : chunk * span + lo + span // ROW_L, col : col + WIN_ONE // COL_L] = made
+                best = jnp.max(made.reshape(LAG_CHUNK // ROW_L, heads, WIN_ONE // COL_L), axis=0)
+                for lane in range(0, WIN_ONE // COL_L, depth):
+                    part = best[:, lane : lane + depth]
+                    top = part if top is None else jnp.maximum(top, part)
+        return top
+
+    chunks = WIN_TWO // LAG_CHUNK
     load_keys(0)
-    s_first[...] = logits(0, 0)
-    lane_pos = lax.broadcasted_iota(jnp.int32, (WIN_ONE, depth), 0)
-
-    def step(token, carry):
+    start_top = None
+    for chunk in range(chunks):
+        start_top = logits(0, chunk, start_top)
+
+    def step(token, top):
         start = lead_one + token - (WIN_ONE - 1)
         vw[:, :depth] = v1f[pl.ds(start, WIN_ONE), :].astype(jnp.bfloat16)
         vw[:, depth:] = jnp.where(lane_pos + start < first_one, 0.0, 1.0).astype(jnp.bfloat16)
-        peak = num = den = None
-        chunks = WIN_TWO // LAG_CHUNK
-        scores = s_first[...]
+        later = jnp.minimum(token + 1, piece - 1)
+        load_keys(later)
+        peak = jnp.max(top, axis=1, keepdims=True)
+        num = den = later_top = None
         for chunk in range(chunks):
-            if chunk + 1 < chunks:
-                following = logits(token, chunk + 1)
-            else:
-                later = jnp.minimum(token + 1, piece - 1)
-                load_keys(later)
-                s_first[...] = logits(later, 0)
-            parts = scores.reshape(LAG_CHUNK, heads, WIN_ONE)
-            top = jnp.max(jnp.max(parts, axis=0), axis=1, keepdims=True)
-            raised_peak = top if peak is None else jnp.maximum(peak, top)
-            raised = jnp.exp(parts - raised_peak[None]).astype(jnp.bfloat16)
-            mixed = jnp.dot(
-                raised.reshape(LAG_CHUNK * heads, WIN_ONE), vw[...], preferred_element_type=jnp.float32
-            )
-            mixed = mixed.reshape(LAG_CHUNK, heads, 2 * depth)
-            if peak is not None:
-                fade = jnp.exp(peak - raised_peak)
-                num = num * fade
-                den = den * fade
-            for index in range(LAG_CHUNK):
-                row = lead_two + token - (chunk * LAG_CHUNK + index)
-                more = mixed[index, :, :depth] * v2f[pl.ds(row, 1), :]
-                count = mixed[index, :, depth:] * one2[pl.ds(row, 1), :]
-                num = more if num is None else num + more
-                den = count if den is None else den + count
-            peak = raised_peak
-            if chunk + 1 < chunks:
-                scores = following
+            sub = LAG_CHUNK // ROW_B
+            for lo in range(0, LAG_CHUNK, sub):
+                base = (chunk * LAG_CHUNK + lo) * heads
+                parts = scores[base : base + sub * heads, :].reshape(sub, heads, WIN_ONE)
+                raised = jnp.exp(parts - peak[None]).astype(jnp.bfloat16)
+                mixed = jnp.dot(
+                    raised.reshape(sub * heads, WIN_ONE), vw[...], preferred_element_type=jnp.float32
+                )
+                mixed = mixed.reshape(sub, heads, 2 * depth)
+                for index in range(sub):
+                    row = lead_two + token - (chunk * LAG_CHUNK + lo + index)
+                    more = mixed[index, :, :depth] * v2f[pl.ds(row, 1), :]
+                    count = mixed[index, :, depth:] * one2[pl.ds(row, 1), :]
+                    num = more if num is None else num + more
+                    den = count if den is None else den + count
+            later_top = logits(later, chunk, later_top)
         out[token] = (num / den).astype(out.dtype)
-        return carry
-
-    lax.fori_loop(0, piece, step, 0)
+        return later_top
+
+    lax.fori_loop(0, piece, step, start_top)
 
 
 def body(queries, key_one, value_one, key_two, value_two):
@@ -208,7 +215,7 @@
             pltpu.VMEM(long_two, jnp.float32),
             pltpu.VMEM((WIN_ONE, depth), jnp.bfloat16),
             pltpu.VMEM((WIN_ONE, 2 * depth), jnp.bfloat16),
-            pltpu.VMEM((LAG_CHUNK * heads, WIN_ONE), jnp.float32),
+            pltpu.VMEM((WIN_TWO * heads, WIN_ONE), jnp.float32),
         ],
         compiler_params=pltpu.CompilerParams(vmem_limit_bytes=48 * 1024 * 1024),
     )(queries, *halos, key_one, value_one, key_two, value_two)

time: 94 us -> 76.2 us (0.81)
  Pallas kernels: 89.1 us -> 71.3 us
    pallas_call x1, Pallas kernels: 74.7 us -> 56.9 us  [body(): pl.pallas_call(attend_kernel, out_shape=jax.ShapeDtypeStruct(queries.shap...]
where the time goes in v2:
time: 76.2 us; the launch traced here: 75.6 us
  Pallas kernels  71.3 us (94%)
  local copies, waits for them, and re-layouts  4.31 us (6%)
    pallas_call x1, Pallas kernels, body(): pl.pallas_call(attend_kernel, out_shape=jax.ShapeDtypeStruct(queries.shap...  56.9 us
    pallas_call x1, Pallas kernels, body(): pl.pallas_call(functools.partial(halo_kernel, reach), out_shape=behind, i...  14.4 us
    unnamed x18, local copies, waits for them, and re-layouts  4.31 us

profile of v2, /device:TPU:4, one launch (start us, length us, event | category | flops | bytes accessed | tf_op | source)
XLA Modules:
  0.0 75.6 jit_solution(761618132978690927)
XLA Ops:
  0.0 0.0 copy-start.3
  0.0 0.0 copy-start.4
  0.0 0.0 copy-start.5
  0.0 0.0 copy-start.6
  0.0 14.4 %shard_map.55 = (bf16[13,40,128]{2,1,0:T(8,128)(2,1)}, bf16[13,40,128]{2,1,0:T(8,128)(2,1)}, bf16[1,40,128]{2,1,0:T(8,128)(2,1)}, bf16[1,40,128]{2,1,0:T(8,128)(2,1)}) custom-call(bf16[40,128]{1,0:T(8,128)(2,1)} %k1.3, bf16[40,128]{1,0:T(8,128)(2,1)} %v1.3, bf16[40,128]{1,0:T(8,128)(2,1)} %k2.3, bf16[40,128]{1,0:T(8,128)(2,1)} %v2.3), custom_call_target="tpu_custom_call" | custom-call | tf_op jit(solution)/shard_map/pallas_call | solution.py:192
  14.4 0.0 copy-done.3
  14.4 0.0 copy-done.4
  14.4 0.0 copy-done.5
  14.4 0.0 copy-done.6
  14.4 0.0 copy-start
  14.4 1.1 %copy-done = bf16[40,64,128]{2,1,0:T(8,128)(2,1)S(1)} copy-done((bf16[40,64,128]{2,1,0:T(8,128)(2,1)S(1)}, bf16[40,64,128]{2,1,0:T(8,128)(2,1)}, u32[]{:S(2)}) %copy-start) | copy-done | bytes 655384
  15.5 0.0 copy-start.1
  15.5 0.9 %copy-done.1 = bf16[13,40,128]{2,1,0:T(8,128)(2,1)S(1)} copy-done((bf16[13,40,128]{2,1,0:T(8,128)(2,1)S(1)}, bf16[13,40,128]{2,1,0:T(8,128)(2,1)}, u32[]{:S(2)}) %copy-start.1) | copy-done | bytes 133144
  16.4 0.0 copy-start.2
  16.4 0.9 %copy-done.2 = bf16[13,40,128]{2,1,0:T(8,128)(2,1)S(1)} copy-done((bf16[13,40,128]{2,1,0:T(8,128)(2,1)S(1)}, bf16[13,40,128]{2,1,0:T(8,128)(2,1)}, u32[]{:S(2)}) %copy-start.2) | copy-done | bytes 133144
  17.3 0.0 copy-start.7
  17.3 0.7 copy-done.7
  18.0 0.0 copy-start.8
  18.0 0.7 copy-done.8
  18.7 56.9 %shard_map.56 = bf16[40,64,128]{2,1,0:T(8,128)(2,1)} custom-call(bf16[40,64,128]{2,1,0:T(8,128)(2,1)S(1)} %copy-done, bf16[13,40,128]{2,1,0:T(8,128)(2,1)S(1)} %copy-done.1, bf16[13,40,128]{2,1,0:T(8,128)(2,1)S(1)} %copy-done.2, bf16[1,40,128]{2,1,0:T(8,128)(2,1)S(1)} %copy-done.7, bf16[1,40,128]{2,1,0:T(8,128)(2,1)S(1)} %copy-done.8, ...), custom_call_target="tpu_custom_call" | custom-call | tf_op jit(solution)/shard_map/pallas_call | solution.py:205
Async XLA Ops:
  0.0 14.4 %copy-start.3 = (bf16[40,128]{1,0:T(8,128)(2,1)S(1)}, bf16[40,128]{1,0:T(8,128)(2,1)}, u32[]{:S(2)}) copy-start(bf16[40,128]{1,0:T(8,128)(2,1)} %k1.3) | copy-start | bytes 30724
  0.0 14.4 %copy-start.4 = (bf16[40,128]{1,0:T(8,128)(2,1)S(1)}, bf16[40,128]{1,0:T(8,128)(2,1)}, u32[]{:S(2)}) copy-start(bf16[40,128]{1,0:T(8,128)(2,1)} %v1.3) | copy-start | bytes 30724
  0.0 14.4 %copy-start.5 = (bf16[40,128]{1,0:T(8,128)(2,1)S(1)}, bf16[40,128]{1,0:T(8,128)(2,1)}, u32[]{:S(2)}) copy-start(bf16[40,128]{1,0:T(8,128)(2,1)} %k2.3) | copy-start | bytes 30724
  0.0 14.4 %copy-start.6 = (bf16[40,128]{1,0:T(8,128)(2,1)S(1)}, bf16[40,128]{1,0:T(8,128)(2,1)}, u32[]{:S(2)}) copy-start(bf16[40,128]{1,0:T(8,128)(2,1)} %v2.3) | copy-start | bytes 30724
  14.4 1.1 %copy-start = (bf16[40,64,128]{2,1,0:T(8,128)(2,1)S(1)}, bf16[40,64,128]{2,1,0:T(8,128)(2,1)}, u32[]{:S(2)}) copy-start(bf16[40,64,128]{2,1,0:T(8,128)(2,1)} %q.1) | copy-start | bytes 1966084
  15.5 0.9 %copy-start.1 = (bf16[13,40,128]{2,1,0:T(8,128)(2,1)S(1)}, bf16[13,40,128]{2,1,0:T(8,128)(2,1)}, u32[]{:S(2)}) copy-start(bf16[13,40,128]{2,1,0:T(8,128)(2,1)} %get-tuple-element.9.k1h) | copy-start | bytes 399364
  16.4 0.9 %copy-start.2 = (bf16[13,40,128]{2,1,0:T(8,128)(2,1)S(1)}, bf16[13,40,128]{2,1,0:T(8,128)(2,1)}, u32[]{:S(2)}) copy-start(bf16[13,40,128]{2,1,0:T(8,128)(2,1)} %get-tuple-element.10.v1h) | copy-start | bytes 399364
  17.3 0.7 copy-start.7
  18.0 0.7 copy-start.8

commit v3 on v2

--- a/solution.py
+++ b/solution.py
@@ -13,7 +13,7 @@
 LAG_CHUNK = 8
 ROW_L = 1
 COL_L = 2
-ROW_B = 2
+ROW_B = 4
 
 
 def pieces_behind(window, rows):
@@ -80,10 +80,23 @@
                 copy.wait_recv()
 
 
-def attend_kernel(
-    q, k1h, v1h, k2h, v2h, k1, v1, k2, v2, out, k1f, v1f, k2f, v2f, one2, kw, vw, scores
-):
+def attend_kernel(*refs):
+    q_far, far, out, q, near, fetched = refs[0], refs[1:9], refs[9], refs[10], refs[11:19], refs[19]
+    k1f, v1f, k2f, v2f, one2, kw, vw, scores = refs[20:]
     piece, heads, depth = q.shape
+    fetches = [
+        pltpu.make_async_copy(source, target, fetched.at[index])
+        for index, (source, target) in enumerate(zip(far, near))
+    ]
+    early = pltpu.make_async_copy(q_far.at[pl.ds(0, 1)], q.at[pl.ds(0, 1)], fetched.at[8])
+    rest = pltpu.make_async_copy(q_far.at[pl.ds(1, piece - 1)], q.at[pl.ds(1, piece - 1)], fetched.at[9])
+    for fetch in fetches:
+        fetch.start()
+    early.start()
+    rest.start()
+    k1h, v1h, k2h, v2h, k1, v1, k2, v2 = near
+    for fetch in fetches:
+        fetch.wait()
     inner = lax.axis_size("head")
     me = lax.axis_index("seq") * inner + lax.axis_index("head")
     lead_one = k1h.shape[0] * piece
@@ -148,6 +161,7 @@
 
     chunks = WIN_TWO // LAG_CHUNK
     load_keys(0)
+    early.wait()
     start_top = None
     for chunk in range(chunks):
         start_top = logits(0, chunk, start_top)
@@ -180,6 +194,7 @@
         out[token] = (num / den).astype(out.dtype)
         return later_top
 
+    rest.wait()
     lax.fori_loop(0, piece, step, start_top)
 
 
@@ -205,9 +220,12 @@
     return pl.pallas_call(
         attend_kernel,
         out_shape=jax.ShapeDtypeStruct(queries.shape, queries.dtype),
-        in_specs=[vmem] * 9,
+        in_specs=[anywhere] * 9,
         out_specs=vmem,
         scratch_shapes=[
+            pltpu.VMEM(queries.shape, queries.dtype),
+            *[pltpu.VMEM(x.shape, x.dtype) for x in (*halos, key_one, value_one, key_two, value_two)],
+            pltpu.SemaphoreType.DMA((10,)),
             pltpu.VMEM(long_one, jnp.float32),
             pltpu.VMEM(long_one, jnp.float32),
             pltpu.VMEM(long_two, jnp.float32),
@@ -217,7 +235,6 @@
             pltpu.VMEM((WIN_ONE, 2 * depth), jnp.bfloat16),
             pltpu.VMEM((WIN_TWO * heads, WIN_ONE), jnp.float32),
         ],
-        compiler_params=pltpu.CompilerParams(vmem_limit_bytes=48 * 1024 * 1024),
     )(queries, *halos, key_one, value_one, key_two, value_two)
 
 

time: 76.2 us -> 73.8 us (0.969)
  local copies, waits for them, and re-layouts: 4.31 us -> 0 us
  Pallas kernels: 71.3 us -> 73.4 us
    unnamed x18 -> x0, local copies, waits for them, and re-layouts: 4.31 us -> none
    pallas_call x1, Pallas kernels: 56.9 us -> 59.2 us  [body(): pl.pallas_call(attend_kernel, out_shape=jax.ShapeDtypeStruct(queries.shap...]
where the time goes in v3:
time: 73.8 us; the launch traced here: 73.4 us
  Pallas kernels  73.4 us (99%)
    pallas_call x1, Pallas kernels, body(): pl.pallas_call(attend_kernel, out_shape=jax.ShapeDtypeStruct(queries.shap...  59.2 us
    pallas_call x1, Pallas kernels, body(): pl.pallas_call(functools.partial(halo_kernel, reach), out_shape=behind, i...  14.2 us

profile of v3, /device:TPU:4, one launch (start us, length us, event | category | flops | bytes accessed | tf_op | source)
XLA Modules:
  0.0 73.4 jit_solution(8414517351019095300)
XLA Ops:
  0.0 14.2 %shard_map.55 = (bf16[13,40,128]{2,1,0:T(8,128)(2,1)}, bf16[13,40,128]{2,1,0:T(8,128)(2,1)}, bf16[1,40,128]{2,1,0:T(8,128)(2,1)}, bf16[1,40,128]{2,1,0:T(8,128)(2,1)}) custom-call(bf16[40,128]{1,0:T(8,128)(2,1)} %refs_5_.1, bf16[40,128]{1,0:T(8,128)(2,1)} %refs_6_.1, bf16[40,128]{1,0:T(8,128)(2,1)} %refs_7_.1, bf16[40,128]{1,0:T(8,128)(2,1)} %refs_8_.1), custom_call_target="tpu_custom_call" | custom-call | tf_op jit(solution)/shard_map/pallas_call | solution.py:207
  14.2 59.2 %shard_map.56 = bf16[40,64,128]{2,1,0:T(8,128)(2,1)} custom-call(bf16[40,64,128]{2,1,0:T(8,128)(2,1)} %refs_0_.1, bf16[13,40,128]{2,1,0:T(8,128)(2,1)} %get-tuple-element.9.refs_1_, bf16[13,40,128]{2,1,0:T(8,128)(2,1)} %get-tuple-element.10.refs_2_, bf16[1,40,128]{2,1,0:T(8,128)(2,1)} %get-tuple-element.11.refs_3_, ...), custom_call_target="tpu_custom_call" | custom-call | tf_op jit(solution)/shard_map/pallas_call | solution.py:220

commit v4 on v3

--- a/solution.py
+++ b/solution.py
@@ -20,70 +20,167 @@
     return (window - 2) // rows + 1
 
 
-def halo_kernel(reach, k1, v1, k2, v2, k1_out, v1_out, k2_out, v2_out, send, recv):
-    inner = lax.axis_size("head")
-    count = lax.axis_size("seq") * inner
-    me = lax.axis_index("seq") * inner + lax.axis_index("head")
-    flows = [(k1, k1_out, reach[0]), (v1, v1_out, reach[0])]
-    flows += [(k2, k2_out, reach[1]), (v2, v2_out, reach[1])]
-    far = max(reach)
-
-    def place(index):
-        return (index // inner, index % inner)
+def shards_behind(reach, inner):
+    return (reach + inner - 1) // inner
+
+
+def halo_kernel(reach, k1, v1, k2, v2, k1_out, v1_out, k2_out, v2_out, *sems):
+    side_send, side_recv, fore_send, fore_recv, near_send, near_recv = sems
+    inner, outer = lax.axis_size("head"), lax.axis_size("seq")
+    seq, col = lax.axis_index("seq"), lax.axis_index("head")
+    me, count = seq * inner + col, outer * inner
+    shards = shards_behind(reach[0], inner)
+    base = shards * inner
+    firsts = ((k1, k1_out), (v1, v1_out))
+    seconds = ((k2, k2_out), (v2, v2_out))
+
+    def remote(source, target, send, recv, where):
+        return pltpu.make_async_remote_copy(
+            src_ref=source,
+            dst_ref=target,
+            send_sem=send,
+            recv_sem=recv,
+            device_id=where,
+            device_id_type=pl.DeviceIdType.MESH,
+        )
+
+    def around(turn):
+        return (col + turn) % inner
+
+    def side(turn):
+        return [
+            remote(
+                source,
+                target.at[base + col],
+                side_send.at[flow, turn - 1],
+                side_recv.at[flow, turn - 1],
+                (seq, around(turn)),
+            )
+            for flow, (source, target) in enumerate(firsts)
+        ]
+
+    def side_arrival(turn):
+        return [
+            remote(
+                source,
+                target.at[base + around(turn)],
+                side_send.at[flow, inner - turn - 1],
+                side_recv.at[flow, inner - turn - 1],
+                (seq, around(turn)),
+            )
+            for flow, (source, target) in enumerate(firsts)
+        ]
+
+    def fore(hop, turn):
+        return [
+            remote(
+                source if turn == 0 else target.at[base + around(turn)],
+                target.at[(shards - hop) * inner + around(turn)],
+                fore_send.at[flow, hop - 1, turn],
+                fore_recv.at[flow, hop - 1, turn],
+                (seq + hop, col),
+            )
+            for flow, (source, target) in enumerate(firsts)
+        ]
+
+    def near(step):
+        there = me + step
+        return [
+            remote(
+                source,
+                target.at[reach[1] - step],
+                near_send.at[flow, step - 1],
+                near_recv.at[flow, step - 1],
+                (there // inner, there % inner),
+            )
+            for flow, (source, target) in enumerate(seconds)
+        ]
+
+    def wanted(hop, turn):
+        return hop * inner <= reach[0] + around(turn) - col
+
+    def greet(where):
+        pl.semaphore_signal(barrier, inc=1, device_id=where, device_id_type=pl.DeviceIdType.MESH)
 
     barrier = pltpu.get_barrier_semaphore()
-    for step in range(1, far + 1):
+    hops = (reach[0] + inner - 1 - col) // inner
+    for turn in range(1, inner):
+        greet((seq, around(turn)))
+    for hop in range(1, shards + 1):
+
+        @pl.when((seq - hop >= 0) & (hop <= hops))
+        def _():
+            greet((seq - hop, col))
+
+    for step in range(1, reach[1] + 1):
 
         @pl.when(me - step >= 0)
         def _():
-            pl.semaphore_signal(
-                barrier, inc=1, device_id=place(me - step), device_id_type=pl.DeviceIdType.MESH
-            )
-
-    @pl.when(me + 1 < count)
-    def _():
-        pl.semaphore_wait(barrier, jnp.minimum(far, count - 1 - me))
-
-    def copies(step):
-        made = []
-        for flow, (source, target, width) in enumerate(flows):
-            if step <= width:
-                made.append(
-                    pltpu.make_async_remote_copy(
-                        src_ref=source,
-                        dst_ref=target.at[width - step],
-                        send_sem=send.at[flow, step - 1],
-                        recv_sem=recv.at[flow, step - 1],
-                        device_id=place(me + step),
-                        device_id_type=pl.DeviceIdType.MESH,
-                    )
-                )
-        return made
-
-    for step in range(far, 0, -1):
+            greet(((me - step) // inner, (me - step) % inner))
+
+    peers = inner - 1 + jnp.minimum(hops, outer - 1 - seq) + jnp.minimum(reach[1], count - 1 - me)
+    pl.semaphore_wait(barrier, peers)
+
+    for turn in range(1, inner):
+        for copy in side(turn):
+            copy.start()
+    for turn in range(inner):
+        if turn:
+            for copy in side_arrival(turn):
+                copy.wait_recv()
+        for hop in range(shards, 0, -1):
+
+            @pl.when((seq + hop < outer) & wanted(hop, turn))
+            def _():
+                for copy in fore(hop, turn):
+                    copy.start()
+
+        if turn == 0:
+            for step in range(1, reach[1] + 1):
+
+                @pl.when(me + step < count)
+                def _():
+                    for copy in near(step):
+                        copy.start()
+
+    for turn in range(inner):
+        for hop in range(shards, 0, -1):
+
+            @pl.when((seq - hop >= 0) & wanted(hop, turn))
+            def _():
+                for copy in fore(hop, turn):
+                    copy.wait_recv()
+
+            @pl.when((seq + hop < outer) & wanted(hop, turn))
+            def _():
+                for copy in fore(hop, turn):
+                    copy.wait_send()
+
+    for step in range(1, reach[1] + 1):
+
+        @pl.when(me - step >= 0)
+        def _():
+            for copy in near(step):
+                copy.wait_recv()
 
         @pl.when(me + step < count)
         def _():
-            for copy in copies(step):
-                copy.start()
-
-    for step in range(far, 0, -1):
-
-        @pl.when(me + step < count)
-        def _():
-            for copy in copies(step):
+            for copy in near(step):
                 copy.wait_send()
 
-        @pl.when(me - step >= 0)
-        def _():
-            for copy in copies(step):
-                copy.wait_recv()
+    for turn in range(1, inner):
+        for copy in side(turn):
+            copy.wait_send()
 
 
 def attend_kernel(*refs):
     q_far, far, out, q, near, fetched = refs[0], refs[1:9], refs[9], refs[10], refs[11:19], refs[19]
     k1f, v1f, k2f, v2f, one2, kw, vw, scores = refs[20:]
     piece, heads, depth = q.shape
+    inner = lax.axis_size("head")
+    reach = near[0].shape[0]
+    skip = lax.axis_index("head") + shards_behind(reach, inner) * inner - reach
+    far = [far[0].at[pl.ds(skip, reach)], far[1].at[pl.ds(skip, reach)], *far[2:]]
     fetches = [
         pltpu.make_async_copy(source, target, fetched.at[index])
         for index, (source, target) in enumerate(zip(far, near))
@@ -203,15 +300,20 @@
     reach = (pieces_behind(WIN_ONE, piece), pieces_behind(WIN_TWO, piece))
     anywhere = pl.BlockSpec(memory_space=pl.ANY)
     vmem = pl.BlockSpec(memory_space=pltpu.VMEM)
-    behind = [jax.ShapeDtypeStruct((r, piece, depth), key_one.dtype) for r in (reach[0], reach[0], reach[1], reach[1])]
+    inner = lax.axis_size("head")
+    shards = shards_behind(reach[0], inner)
+    slots = (shards + 1) * inner
+    behind = [jax.ShapeDtypeStruct((r, piece, depth), key_one.dtype) for r in (slots, slots, reach[1], reach[1])]
+    windows = [jax.ShapeDtypeStruct((r, piece, depth), key_one.dtype) for r in (reach[0], reach[0], reach[1], reach[1])]
     halos = pl.pallas_call(
         functools.partial(halo_kernel, reach),
         out_shape=behind,
         in_specs=[anywhere] * 4,
         out_specs=[anywhere] * 4,
         scratch_shapes=[
-            pltpu.SemaphoreType.DMA((4, max(reach))),
-            pltpu.SemaphoreType.DMA((4, max(reach))),
+            *[pltpu.SemaphoreType.DMA((2, inner))] * 2,
+            *[pltpu.SemaphoreType.DMA((2, shards, inner))] * 2,
+            *[pltpu.SemaphoreType.DMA((2, reach[1]))] * 2,
         ],
         compiler_params=pltpu.CompilerParams(collective_id=0, has_side_effects=True),
     )(key_one, value_one, key_two, value_two)
@@ -224,7 +326,7 @@
         out_specs=vmem,
         scratch_shapes=[
             pltpu.VMEM(queries.shape, queries.dtype),
-            *[pltpu.VMEM(x.shape, x.dtype) for x in (*halos, key_one, value_one, key_two, value_two)],
+            *[pltpu.VMEM(x.shape, x.dtype) for x in (*windows, key_one, value_one, key_two, value_two)],
             pltpu.SemaphoreType.DMA((10,)),
             pltpu.VMEM(long_one, jnp.float32),
             pltpu.VMEM(long_one, jnp.float32),

time: 73.8 us -> 71.5 us (0.969)
  Pallas kernels: 73.4 us -> 71.3 us
    pallas_call x1, Pallas kernels: 14.2 us -> 12.1 us  [body(): pl.pallas_call(functools.partial(halo_kernel, reach), out_shape=behind, i...]
where the time goes in v4:
time: 71.5 us; the launch traced here: 71.4 us
  Pallas kernels  71.3 us (100%)
    pallas_call x1, Pallas kernels, body(): pl.pallas_call(attend_kernel, out_shape=jax.ShapeDtypeStruct(queries.shap...  59.2 us
    pallas_call x1, Pallas kernels, body(): pl.pallas_call(functools.partial(halo_kernel, reach), out_shape=behind, i...  12.1 us

profile of v4, /device:TPU:4, one launch (start us, length us, event | category | flops | bytes accessed | tf_op | source)
XLA Modules:
  0.0 71.4 jit_solution(6144467997275867951)
XLA Ops:
  0.0 12.1 %shard_map.55 = (bf16[20,40,128]{2,1,0:T(8,128)(2,1)}, bf16[20,40,128]{2,1,0:T(8,128)(2,1)}, bf16[1,40,128]{2,1,0:T(8,128)(2,1)}, bf16[1,40,128]{2,1,0:T(8,128)(2,1)}) custom-call(bf16[40,128]{1,0:T(8,128)(2,1)} %refs_5_.1, bf16[40,128]{1,0:T(8,128)(2,1)} %refs_6_.1, bf16[40,128]{1,0:T(8,128)(2,1)} %refs_7_.1, bf16[40,128]{1,0:T(8,128)(2,1)} %refs_8_.1), custom_call_target="tpu_custom_call" | custom-call | tf_op jit(solution)/shard_map/pallas_call | solution.py:308
  12.1 59.2 %shard_map.56 = bf16[40,64,128]{2,1,0:T(8,128)(2,1)} custom-call(bf16[40,64,128]{2,1,0:T(8,128)(2,1)} %refs_0_.1, bf16[20,40,128]{2,1,0:T(8,128)(2,1)} %get-tuple-element.9.refs_1_, bf16[20,40,128]{2,1,0:T(8,128)(2,1)} %get-tuple-element.10.refs_2_, bf16[1,40,128]{2,1,0:T(8,128)(2,1)} %get-tuple-element.11.refs_3_, ...), custom_call_target="tpu_custom_call" | custom-call | tf_op jit(solution)/shard_map/pallas_call | solution.py:322

commit v5 on v4

--- a/solution.py
+++ b/solution.py
@@ -231,10 +231,10 @@
     span = LAG_CHUNK * heads
     lane_pos = lax.broadcasted_iota(jnp.int32, (WIN_ONE, depth), 0)
 
-    def load_keys(token):
-        kw[...] = k1f[pl.ds(lead_one + token - (WIN_ONE - 1), WIN_ONE), :].astype(jnp.bfloat16)
-
-    def logits(token, chunk, top):
+    def load_keys(token, slot):
+        kw[slot] = k1f[pl.ds(lead_one + token - (WIN_ONE - 1), WIN_ONE), :].astype(jnp.bfloat16)
+
+    def logits(token, chunk, top, slot):
         query = q[token].astype(jnp.float32)
         rows = []
         for lag in range(chunk * LAG_CHUNK, (chunk + 1) * LAG_CHUNK):
@@ -245,7 +245,7 @@
             for col in range(0, WIN_ONE, WIN_ONE // COL_L):
                 made = lax.dot_general(
                     product[lo : lo + span // ROW_L],
-                    kw[col : col + WIN_ONE // COL_L, :],
+                    kw[slot, col : col + WIN_ONE // COL_L, :],
                     (((1,), (1,)), ((), ())),
                     preferred_element_type=jnp.float32,
                 )
@@ -257,28 +257,32 @@
         return top
 
     chunks = WIN_TWO // LAG_CHUNK
-    load_keys(0)
+    load_keys(0, 0)
     early.wait()
     start_top = None
     for chunk in range(chunks):
-        start_top = logits(0, chunk, start_top)
-
-    def step(token, top):
+        start_top = logits(0, chunk, start_top, 0)
+
+    def step(token, top, slot):
         start = lead_one + token - (WIN_ONE - 1)
-        vw[:, :depth] = v1f[pl.ds(start, WIN_ONE), :].astype(jnp.bfloat16)
-        vw[:, depth:] = jnp.where(lane_pos + start < first_one, 0.0, 1.0).astype(jnp.bfloat16)
+        vw[slot, :, :depth] = v1f[pl.ds(start, WIN_ONE), :].astype(jnp.bfloat16)
+        vw[slot, :, depth:] = jnp.where(lane_pos + start < first_one, 0.0, 1.0).astype(jnp.bfloat16)
         later = jnp.minimum(token + 1, piece - 1)
-        load_keys(later)
+        load_keys(later, 1 - slot)
         peak = jnp.max(top, axis=1, keepdims=True)
         num = den = later_top = None
-        for chunk in range(chunks):
+        def weigh(chunk):
+            base = chunk * span
+            parts = scores[base : base + span, :].reshape(LAG_CHUNK, heads, WIN_ONE)
+            return jnp.exp(parts - peak[None]).astype(jnp.bfloat16)
+
+        def blend(chunk, raised, num, den):
             sub = LAG_CHUNK // ROW_B
             for lo in range(0, LAG_CHUNK, sub):
-                base = (chunk * LAG_CHUNK + lo) * heads
-                parts = scores[base : base + sub * heads, :].reshape(sub, heads, WIN_ONE)
-                raised = jnp.exp(parts - peak[None]).astype(jnp.bfloat16)
                 mixed = jnp.dot(
-                    raised.reshape(sub * heads, WIN_ONE), vw[...], preferred_element_type=jnp.float32
+                    raised[lo : lo + sub].reshape(sub * heads, WIN_ONE),
+                    vw[slot],
+                    preferred_element_type=jnp.float32,
                 )
                 mixed = mixed.reshape(sub, heads, 2 * depth)
                 for index in range(sub):
@@ -287,12 +291,28 @@
                     count = mixed[index, :, depth:] * one2[pl.ds(row, 1), :]
                     num = more if num is None else num + more
                     den = count if den is None else den + count
-            later_top = logits(later, chunk, later_top)
+            return num, den
+
+        for chunk in range(chunks):
+            raised = weigh(chunk)
+            if chunk + 1 < chunks:
+                num, den = blend(chunk, raised, num, den)
+                later_top = logits(later, chunk, later_top, 1 - slot)
+            else:
+                later_top = logits(later, chunk, later_top, 1 - slot)
+                num, den = blend(chunk, raised, num, den)
         out[token] = (num / den).astype(out.dtype)
         return later_top
 
     rest.wait()
-    lax.fori_loop(0, piece, step, start_top)
+    unroll = math.gcd(piece, 2)
+
+    def several(index, top):
+        for turn in range(unroll):
+            top = step(index * unroll + turn, top, turn % 2 if unroll > 1 else 0)
+        return top
+
+    lax.fori_loop(0, piece // unroll, several, start_top)
 
 
 def body(queries, key_one, value_one, key_two, value_two):
@@ -333,8 +353,8 @@
             pltpu.VMEM(long_two, jnp.float32),
             pltpu.VMEM(long_two, jnp.float32),
             pltpu.VMEM(long_two, jnp.float32),
-            pltpu.VMEM((WIN_ONE, depth), jnp.bfloat16),
-            pltpu.VMEM((WIN_ONE, 2 * depth), jnp.bfloat16),
+            pltpu.VMEM((2, WIN_ONE, depth), jnp.bfloat16),
+            pltpu.VMEM((2, WIN_ONE, 2 * depth), jnp.bfloat16),
             pltpu.VMEM((WIN_TWO * heads, WIN_ONE), jnp.float32),
         ],
     )(queries, *halos, key_one, value_one, key_two, value_two)

time: 71.5 us -> 68.6 us (0.959)
  Pallas kernels: 71.3 us -> 68.4 us
    pallas_call x1, Pallas kernels: 59.2 us -> 56.3 us  [body(): pl.pallas_call(attend_kernel, out_shape=jax.ShapeDtypeStruct(queries.shap...]
where the time goes in v5:
time: 68.6 us; the launch traced here: 68.4 us
  Pallas kernels  68.4 us (100%)
    pallas_call x1, Pallas kernels, body(): pl.pallas_call(attend_kernel, out_shape=jax.ShapeDtypeStruct(queries.shap...  56.3 us
    pallas_call x1, Pallas kernels, body(): pl.pallas_call(functools.partial(halo_kernel, reach), out_shape=behind, i...  12.1 us

profile of v5, /device:TPU:4, one launch (start us, length us, event | category | flops | bytes accessed | tf_op | source)
XLA Modules:
  0.0 68.4 jit_solution(442490248581606920)
XLA Ops:
  0.0 12.1 %shard_map.55 = (bf16[20,40,128]{2,1,0:T(8,128)(2,1)}, bf16[20,40,128]{2,1,0:T(8,128)(2,1)}, bf16[1,40,128]{2,1,0:T(8,128)(2,1)}, bf16[1,40,128]{2,1,0:T(8,128)(2,1)}) custom-call(bf16[40,128]{1,0:T(8,128)(2,1)} %refs_5_.1, bf16[40,128]{1,0:T(8,128)(2,1)} %refs_6_.1, bf16[40,128]{1,0:T(8,128)(2,1)} %refs_7_.1, bf16[40,128]{1,0:T(8,128)(2,1)} %refs_8_.1), custom_call_target="tpu_custom_call" | custom-call | tf_op jit(solution)/shard_map/pallas_call | solution.py:328
  12.1 56.3 %shard_map.56 = bf16[40,64,128]{2,1,0:T(8,128)(2,1)} custom-call(bf16[40,64,128]{2,1,0:T(8,128)(2,1)} %refs_0_.1, bf16[20,40,128]{2,1,0:T(8,128)(2,1)} %get-tuple-element.9.refs_1_, bf16[20,40,128]{2,1,0:T(8,128)(2,1)} %get-tuple-element.10.refs_2_, bf16[1,40,128]{2,1,0:T(8,128)(2,1)} %get-tuple-element.11.refs_3_, ...), custom_call_target="tpu_custom_call" | custom-call | tf_op jit(solution)/shard_map/pallas_call | solution.py:342
